TPU v7x, 32 devices: a whole 2x2x4 slice. The times are simulated.
32 devices in a mesh: dom: 16 (over z, y, core), feat: 2 (over x).
Axes of the slice: x: 2, y: 2, z: 4, core: 2. Of those that a mesh axis runs over, the one named last changes fastest.
Arguments:
- features: bfloat16 [256, 8192], P('feat', 'dom'), may hold values from -6 to 6
- in_degree: int32 [8192], P('dom'), may hold values from 16 to 64
- send_rows: int32 [16, 16, 16], P('dom'), may hold values from 0 to 511
- send_count: int32 [16, 16], P('dom'), may hold values from 0 to 16, as said below
- hub_owner: int32 [4], replicated, may hold values from 0 to 15, as said below
- hub_rows: int32 [4, 128], replicated, may hold values from 0 to 511
- local_dest: int32 [256], P('dom'), may hold values from 0 to 3
- local_source: int32 [256], P('dom'), may hold values from 0 to 3
- local_tiles: bfloat16 [256, 128, 128], P('dom'), may hold values from 0 to 1
- border_dest: int32 [256], P('dom'), may hold values from 0 to 3
- border_source: int32 [256], P('dom'), may hold values from 0 to 1
- border_tiles: bfloat16 [256, 128, 128], P('dom'), may hold values from 0 to 1
- hub_dest: int32 [256], P('dom'), may hold values from 0 to 3
- hub_source: int32 [256], P('dom'), may hold values from 0 to 3
- hub_tiles: bfloat16 [256, 128, 128], P('dom'), may hold values from 0 to 1
- self_weight: bfloat16 [256, 256], P('feat'), may hold values from -0.375 to 0.375
- neighbor_weight: bfloat16 [256, 256], P('feat'), may hold values from -0.375 to 0.375
- out_bias: float32 [256], P('feat'), may hold values from -3 to 3
Outputs:
- updated: bfloat16 [256, 8192], P('feat', 'dom')
Inputs may be any that keep to these rules, and one draw needn't show every extreme that they name: send_count[q, p] of the 16 slots from q to p are live; in every draw some destinations receive 16 live rows from every source. Hub block b belongs to partition hub_owner[b]; one partition owns exactly 2 blocks, every other partition at most one.
All inputs are finite; a program needn't handle non-finite values.
Results may differ from a plain program's by a relative error of at most 0.0034.
Values may be sent and summed in bfloat16 or wider, within the bound.
No kernel may reach another device: no remote copies, remote signals or barrier semaphores. Data moves between devices by JAX's collectives and lax.ppermute only.
A program may use at most 64 MiB of HBM per device.

v0:
```python
import jax
import jax.numpy as jnp
from jax import lax
from jax.sharding import PartitionSpec as P

HOWN = 2


def tile_terms(blocks, targets, source, tile_values, row_blocks):
    picked = jnp.take(blocks, source, axis=1)
    partial_value = jnp.einsum(
        "ftk,tik->fti", picked, tile_values, preferred_element_type=jnp.float32
    )
    onehot = (targets[:, None] == jnp.arange(row_blocks, dtype=jnp.int32)[None, :]).astype(
        jnp.float32
    )
    return jnp.einsum("fti,tr->fri", partial_value, onehot, precision=lax.Precision.HIGHEST)


def shards(
    features,
    in_degree,
    send_rows,
    send_count,
    hub_owner,
    hub_rows,
    local_dest,
    local_source,
    local_tiles,
    border_dest,
    border_source,
    border_tiles,
    hub_dest,
    hub_source,
    hub_tiles,
    self_weight,
    neighbor_weight,
    out_bias,
):
    feat_rows, vertex_count = features.shape
    tile_size = local_tiles.shape[1]
    row_blocks = vertex_count // tile_size
    partitions = lax.axis_size("dom")
    capacity = send_rows.shape[2]
    own_blocks = features.reshape(feat_rows, row_blocks, tile_size)
    local_sum = tile_terms(own_blocks, local_dest, local_source, local_tiles, row_blocks)
    pick_rows = send_rows[0].reshape(-1)
    outgoing = jnp.take(features, pick_rows, axis=1).reshape(feat_rows, partitions, capacity)
    alive_slots = (jnp.arange(capacity, dtype=jnp.int32)[None, :] < send_count[0][:, None]).astype(
        jnp.bfloat16
    )
    outgoing = outgoing * alive_slots[None]
    incoming = lax.all_to_all(outgoing, "dom", split_axis=1, concat_axis=1, tiled=True)
    border_blocks = incoming.reshape(feat_rows, partitions * capacity // tile_size, tile_size)
    border_sum = tile_terms(border_blocks, border_dest, border_source, border_tiles, row_blocks)
    hub_count = hub_owner.shape[0]
    position = lax.axis_index("dom")
    block_ids = jnp.arange(hub_count, dtype=jnp.int32)
    earlier = block_ids[:, None] > block_ids[None, :]
    same_owner = hub_owner[:, None] == hub_owner[None, :]
    order_rank = jnp.sum((earlier & same_owner).astype(jnp.int32), axis=1)
    owned_here = hub_owner == position
    choose = (
        owned_here[None, :] & (order_rank[None, :] == jnp.arange(HOWN, dtype=jnp.int32)[:, None])
    ).astype(jnp.int32)
    slot_rows = jnp.sum(choose[:, :, None] * hub_rows[None], axis=1)
    owned_blocks = jnp.take(features, slot_rows.reshape(-1), axis=1).reshape(
        feat_rows, HOWN, tile_size
    )
    everyone = lax.all_gather(owned_blocks, "dom", axis=1, tiled=True)
    hub_blocks = jnp.take(everyone, hub_owner * HOWN + order_rank, axis=1)
    hub_sum = tile_terms(hub_blocks, hub_dest, hub_source, hub_tiles, row_blocks)
    degree = in_degree.astype(jnp.float32).reshape(row_blocks, tile_size)
    aggregate = (
        ((local_sum + border_sum + hub_sum) / degree[None])
        .astype(jnp.bfloat16)
        .reshape(feat_rows, vertex_count)
    )
    running = jnp.dot(
        self_weight,
        lax.all_gather(features, "feat", axis=0, tiled=True),
        preferred_element_type=jnp.float32,
    )
    combined = running + jnp.dot(
        neighbor_weight,
        lax.all_gather(aggregate, "feat", axis=0, tiled=True),
        preferred_element_type=jnp.float32,
    )
    return jnp.maximum(combined + out_bias[:, None], 0.0).astype(jnp.bfloat16)


def solution(mesh):
    placed = (
        P("feat", "dom"),
        P("dom"),
        P("dom", None, None),
        P("dom", None),
        P(),
        P(),
        P("dom"),
        P("dom"),
        P("dom", None, None),
        P("dom"),
        P("dom"),
        P("dom", None, None),
        P("dom"),
        P("dom"),
        P("dom", None, None),
        P("feat", None),
        P("feat", None),
        P("feat"),
    )
    return jax.shard_map(
        shards, mesh=mesh, in_specs=placed, out_specs=P("feat", "dom"), check_vma=False
    )
```

profile of v0, /device:TPU:0, one launch (start us, length us, event | category | flops | bytes accessed | tf_op | source)
XLA Modules:
  0.0 80.8 jit_solution(9627374421501627303)
XLA Ops:
  6.5 0.8 %reshape_squeeze.3 = s32[256]{0:T(256)S(1)} reshape(s32[1,16,16]{2,1,0:T(8,128)} %param.24) | data formatting | bytes 2048 | tf_op jit(solution)/shard_map/reshape;squeeze | solution.py:47
  7.4 1.0 %copy.61 = bf16[128,512]{0,1:T(8,128)(2,1)S(1)} copy(bf16[128,512]{1,0:T(8,128)(2,1)} %param.22) | data formatting | bytes 262144 | tf_op args[0]
  8.4 0.0 copy-start.11
  8.4 0.6 copy-done.11
  9.1 0.1 fusion.21
  9.2 0.9 %gather_fusion.3 = bf16[256,128]{1,0:T(8,128)(2,1)S(1)} fusion(bf16[128,512]{0,1:T(8,128)(2,1)S(1)} %copy.61, s32[1024]{0:T(1024)S(1)} %pad_clamp_fusion.4), kind=kCustom, calls=%fused_computation.1.clone | custom fusion | bytes 132096 | tf_op jit(solution)/shard_map/jit(_take)/gather | solution.py:48
  10.0 0.1 broadcast_select_fusion.1
  10.1 0.7 broadcast_multiply_fusion
  10.9 7.4 %all-to-all-start = ((bf16[128,16,16]{0,2,1:T(8,128)(2,1)}), bf16[128,16,16]{0,2,1:T(8,128)(2,1)S(1)}, u32[]{:S(2)}, u32[]{:S(2)}) async-start(bf16[128,16,16]{0,2,1:T(8,128)(2,1)} %broadcast_multiply_fusion), calls=%async_computation | async-start | bytes 131072 | tf_op jit(solution)/shard_map/all_to_all | solution.py:53
  18.3 0.0 copy-start.12
  18.3 0.0 all-gather.2.cloned.1.call-start
  18.3 0.6 copy-done.12
  18.9 0.2 convert_reduce_fusion
  19.1 0.0 copy-start.6
  19.1 0.7 copy-done.6
  19.8 0.1 multiply_reduce_fusion
  19.9 0.9 %gather_fusion.4 = bf16[256,128]{1,0:T(8,128)(2,1)S(1)} fusion(bf16[128,512]{0,1:T(8,128)(2,1)S(1)} %copy.61, s32[1024]{0:T(1024)S(1)} %pad_clamp_fusion.2), kind=kCustom, calls=%fused_computation.3.clone | custom fusion | bytes 132096 | tf_op jit(solution)/shard_map/jit(_take)/gather | solution.py:67
  20.8 0.1 broadcast_select_fusion
  20.9 0.7 copy.68
  21.6 0.0 all-gather.2.cloned.1.call-update
  21.6 0.6 copy-done.13
  22.3 0.6 copy-done.14
  23.0 0.1 copy.62
  23.1 0.6 gather_fusion.2
  23.8 0.0 copy-start.7
  23.8 0.6 copy-done.7
  24.5 0.5 convolution_bitcast_fusion.2
  25.0 0.1 copy-done.8
  25.1 1.1 %fusion.7 = f32[4,128,128]{2,0,1:T(4,128)S(1)} fusion(f32[128,16,128]{2,0,1:T(8,128)S(1)} %convolution_bitcast_fusion.2, s32[16]{0:T(128)S(1)} %copy-done.8), kind=kOutput, calls=%fused_computation.20 | convolution fusion | flops 12582976 | bytes 1310784 | tf_op jit(solution)/shard_map/fti,tr->fri/dot_general | solution.py:17
  26.2 6.5 %all_gather.9 = bf16[256,512]{1,0:T(8,128)(2,1)S(1)} all-gather(bf16[128,512]{1,0:T(8,128)(2,1)S(1)} %copy-done.3), channel_id=1, replica_groups=mesh['dom'=16,'feat'=2] {'feat'}, dimensions={0}, use_global_device_ids=true | all-gather | bytes 393216 | tf_op jit(solution)/shard_map/all_gather | solution.py:81
  32.7 0.1 copy.65
  32.9 0.6 gather_fusion
  33.5 0.4 copy-done.1
  33.9 0.5 convolution_bitcast_fusion.1
  34.4 0.1 copy-done.9
  34.6 1.1 %convolution_add_fusion.1 = f32[4,128,128]{2,0,1:T(4,128)S(1)} fusion(f32[4,128,128]{2,0,1:T(4,128)S(1)} %fusion.7, f32[128,16,128]{2,0,1:T(8,128)S(1)} %convolution_bitcast_fusion.1, s32[16]{0:T(128)S(1)} %copy-done.9), kind=kOutput, calls=%fused_computation.10 | convolution fusion | flops 12648512 | bytes 1572928 | tf_op jit(solution)/shard_map/fti,tr->fri/dot_general | solution.py:17
  35.6 25.4 %all-gather.2.cloned.1.call-done = bf16[128,32,128]{2,0,1:T(8,128)(2,1)} async-done(((bf16[128,2,128]{2,0,1:T(8,128)(2,1)}), bf16[128,32,128]{2,0,1:T(8,128)(2,1)}) %all-gather.2.cloned.1.call-update) | async-done | bytes 1048592 | tf_op jit(solution)/shard_map/all_gather | solution.py:70
  61.0 1.8 %gather_fusion.1 = bf16[4,128,128]{2,1,0:T(8,128)(2,1)S(1)} fusion(bf16[128,32,128]{2,0,1:T(8,128)(2,1)} %all-gather.2.cloned.1.call-done, s32[1024]{0:T(1024)S(1)} %pad_clamp_fusion.1), kind=kCustom, calls=%fused_computation.5 | custom fusion | bytes 262160 | tf_op jit(solution)/shard_map/jit(_take)/gather | solution.py:71
  62.8 0.1 select_bitcast_fusion
  62.9 0.6 gather_fusion.5
  63.6 0.4 copy-done.2
  64.0 0.5 convolution_bitcast_fusion
  64.5 0.1 copy-done.16
  64.6 1.1 %fusion.3 = bf16[4,128,128]{2,0,1:T(4,128)(2,1)S(1)} fusion(f32[4,128,128]{2,0,1:T(4,128)S(1)} %convolution_add_fusion.1, f32[128,16,128]{2,0,1:T(8,128)S(1)} %convolution_bitcast_fusion, f32[4,128]{1,0:T(4,128)S(1)} %convert_bitcast_fusion, s32[16]{0:T(128)S(1)} %copy-done.16), kind=kOutput, calls=%fused_computation.16 | convolution fusion | flops 12779584 | bytes 1443904 | tf_op jit(solution)/shard_map/fti,tr->fri/dot_general | solution.py:17
  65.7 6.5 %all_gather.11 = bf16[256,512]{1,0:T(8,128)(2,1)S(1)} all-gather(bf16[128,512]{1,0:T(8,128)(2,1)S(1)} %bitcast.56), channel_id=1, replica_groups=mesh['dom'=16,'feat'=2] {'feat'}, dimensions={0}, use_global_device_ids=true | all-gather | bytes 393216 | tf_op jit(solution)/shard_map/all_gather | solution.py:86
  72.2 0.2 convolution_bitcast_fusion.3
  72.4 0.6 copy-done.5
  73.1 0.8 %fusion.4 = bf16[128,512]{1,0:T(8,128)(2,1)} fusion(f32[128,512]{1,0:T(8,128)S(1)} %convolution_bitcast_fusion.3, bf16[128,256]{1,0:T(8,128)(2,1)S(1)} %copy-done.5, bf16[256,512]{1,0:T(8,128)(2,1)S(1)} %all_gather.9, f32[128]{0:T(128)S(1)} %copy-done.10), kind=kOutput, calls=%fused_computation.17 | convolution fusion | flops 33816576 | bytes 721408 | tf_op jit(solution)/shard_map/dot_general | solution.py:79
  (39 shorter events, 0.2 us)
Async XLA Ops:
  6.5 17.9 %copy-start = (bf16[16,128,128]{2,1,0:T(8,128)(2,1)S(1)}, bf16[16,128,128]{2,1,0:T(8,128)(2,1)}, u32[]{:S(2)}) copy-start(bf16[16,128,128]{2,1,0:T(8,128)(2,1)} %param.30) | copy-start | bytes 1572868
  8.4 0.7 copy-start.11
  10.9 21.9 %all-to-all-start = ((bf16[128,16,16]{0,2,1:T(8,128)(2,1)}), bf16[128,16,16]{0,2,1:T(8,128)(2,1)S(1)}, u32[]{:S(2)}, u32[]{:S(2)}) async-start(bf16[128,16,16]{0,2,1:T(8,128)(2,1)} %broadcast_multiply_fusion), calls=%async_computation | async-start | bytes 131072 | tf_op jit(solution)/shard_map/all_to_all | solution.py:53
  18.3 0.7 copy-start.12
  18.3 42.8 %all-gather.2.cloned.1.call-start = ((), (), s32[]{:S(2)}) async-start(), calls=%async_computation.1 | async-start | bytes 1114112 | tf_op jit(solution)/shard_map/all_gather | solution.py:70
  19.1 0.7 copy-start.6
  21.6 0.7 copy-start.13
  22.3 0.7 copy-start.14
  23.1 0.7 copy-start.15
  23.8 0.7 copy-start.7
  24.5 0.7 copy-start.8
  25.1 1.1 %copy-start.3 = (bf16[128,512]{1,0:T(8,128)(2,1)S(1)}, bf16[128,512]{1,0:T(8,128)(2,1)}, u32[]{:S(2)}) copy-start(bf16[128,512]{1,0:T(8,128)(2,1)} %param.22) | copy-start | bytes 393220
  32.9 1.0 %copy-start.1 = (bf16[16,128,128]{2,1,0:T(8,128)(2,1)S(1)}, bf16[16,128,128]{2,1,0:T(8,128)(2,1)}, u32[]{:S(2)}) copy-start(bf16[16,128,128]{2,1,0:T(8,128)(2,1)} %param.33) | copy-start | bytes 1572868
  33.9 0.7 copy-start.9
  62.9 1.0 %copy-start.2 = (bf16[16,128,128]{2,1,0:T(8,128)(2,1)S(1)}, bf16[16,128,128]{2,1,0:T(8,128)(2,1)}, u32[]{:S(2)}) copy-start(bf16[16,128,128]{2,1,0:T(8,128)(2,1)} %param.36) | copy-start | bytes 1572868
  64.0 0.7 copy-start.16
  65.7 6.5 %copy-start.4 = (bf16[128,256]{1,0:T(8,128)(2,1)S(1)}, bf16[128,256]{1,0:T(8,128)(2,1)}, u32[]{:S(2)}) copy-start(bf16[128,256]{1,0:T(8,128)(2,1)} %param.38) | copy-start | bytes 196612
  72.2 0.8 %copy-start.5 = (bf16[128,256]{1,0:T(8,128)(2,1)S(1)}, bf16[128,256]{1,0:T(8,128)(2,1)}, u32[]{:S(2)}) copy-start(bf16[128,256]{1,0:T(8,128)(2,1)} %param.37) | copy-start | bytes 196612
  72.2 0.8 %copy-start.10 = (f32[128]{0:T(128)S(1)}, f32[128]{0:T(128)}, u32[]{:S(2)}) copy-start(f32[128]{0:T(128)} %param.39) | copy-start | bytes 1540
Sparse Core Ops, SparseCore 0:
  21.7 39.2 all-gather.1
where the time goes:
time: 81.3 us; the launch traced here: 80.8 us
  waiting for transfers between devices  25.4 us (31%)
  local copies, waits for them, and re-layouts  14 us (17%)
  between operations  13.7 us (17%)
  blocking collectives  13 us (16%)
  starting transfers between devices  7.43 us (9%)
  matrix products  5.75 us (7%)
  other arithmetic  1.48 us (2%)
    all_gather x1, waiting for transfers between devices, shards(): everyone = lax.all_gather(owned_blocks, 'dom', axis=1, tiled=True)  25.4 us
    all_to_all x1, starting transfers between devices, shards(): lax.all_to_all(outgoing, 'dom', split_axis=1, concat_axis=1, tiled=True)  7.38 us
    unnamed x36, local copies, waits for them, and re-layouts  6.71 us
    all_gather x1, blocking collectives, shards(): lax.all_gather(features, 'feat', axis=0, tiled=True)  6.51 us
    all_gather x1, blocking collectives, shards(): lax.all_gather(aggregate, 'feat', axis=0, tiled=True)  6.47 us
    dot_general x3, matrix products, tile_terms(): jnp.einsum('fti,tr->fri', partial_value, onehot, precision=lax.Precision....  3.16 us
    gather x3, local copies, waits for them, and re-layouts, tile_terms(): picked = jnp.take(blocks, source, axis=1)  1.94 us
    gather x1, local copies, waits for them, and re-layouts, shards(): hub_blocks = jnp.take(everyone, hub_owner * HOWN + order_rank, axis=1)  1.79 us
  transfers between devices with their start and end apart: 2, of which 1 were waited for; matrix products, arithmetic and copies ran while one was open for 8% of the time, Pallas kernels for 0%

commit v1 on v0

--- a/solution.py
+++ b/solution.py
@@ -4,6 +4,18 @@
 from jax.sharding import PartitionSpec as P
 
 HOWN = 2
+
+
+def cut_along(value, dim, peers):
+    shape = value.shape
+    blocks = value.reshape(*shape[:dim], peers, shape[dim] // peers, *shape[dim + 1 :])
+    return jnp.moveaxis(blocks, dim, 0)
+
+
+def laid_out(pieces, dim):
+    shape = list(pieces.shape[1:])
+    shape[dim] *= pieces.shape[0]
+    return jnp.moveaxis(pieces, 0, dim).reshape(shape)
 
 
 def tile_terms(blocks, targets, source, tile_values, row_blocks):
@@ -50,7 +62,14 @@
         jnp.bfloat16
     )
     outgoing = outgoing * alive_slots[None]
-    incoming = lax.all_to_all(outgoing, "dom", split_axis=1, concat_axis=1, tiled=True)
+    devices, index = (lax.axis_size("dom"), lax.axis_index("dom"))
+    blocks_2 = cut_along(outgoing, 1, devices)
+    finished = [blocks_2[index]]
+    for turn in range(1, devices):
+        sent = blocks_2[index ^ turn]
+        finished.append(lax.ppermute(sent, "dom", [(i, i ^ turn) for i in range(devices)]))
+    blocks_2 = jnp.stack(finished)[index ^ jnp.arange(devices)]
+    incoming = laid_out(blocks_2, 1)
     border_blocks = incoming.reshape(feat_rows, partitions * capacity // tile_size, tile_size)
     border_sum = tile_terms(border_blocks, border_dest, border_source, border_tiles, row_blocks)
     hub_count = hub_owner.shape[0]

time: 81.3 us -> 77.9 us (0.958)
  waiting for transfers between devices: 25.4 us -> 7.17 us
  starting transfers between devices: 7.43 us -> 22.1 us
    all_gather x1, waiting for transfers between devices: 25.4 us -> 1.48 us  [shards(): everyone = lax.all_gather(owned_blocks, 'dom', axis=1, tiled=True)]
    ppermute x0 -> x15, starting transfers between devices: none -> 22.1 us  [shards(): lax.ppermute(sent, 'dom', [(i, i ^ turn) for i in range(devices)])]
    all_to_all x1 -> x0, starting transfers between devices: 7.38 us -> none  [shards(): lax.all_to_all(outgoing, 'dom', split_axis=1, concat_axis=1, tiled=True)]
    ppermute x0 -> x15, waiting for transfers between devices: none -> 5.68 us  [shards(): lax.ppermute(sent, 'dom', [(i, i ^ turn) for i in range(devices)])]
    unnamed x36 -> x53, local copies, waits for them, and re-layouts: 6.71 us -> 7.53 us
  transfers between devices with their start and end apart: 2 -> 16, of which waited for: 1 -> 3; matrix products, arithmetic and copies ran while one was open for 8% -> 9% of each run, Pallas kernels for 0% -> 0%
where the time goes in v1:
time: 77.9 us; the launch traced here: 77.4 us
  starting transfers between devices  22.1 us (28%)
  local copies, waits for them, and re-layouts  14.7 us (19%)
  between operations  13.9 us (18%)
  blocking collectives  12.9 us (17%)
  waiting for transfers between devices  7.17 us (9%)
  matrix products  5.77 us (7%)
  other arithmetic  0.82 us (1%)
    ppermute x15, starting transfers between devices, shards(): lax.ppermute(sent, 'dom', [(i, i ^ turn) for i in range(devices)])  22.1 us
    unnamed x53, local copies, waits for them, and re-layouts  7.53 us
    all_gather x1, blocking collectives, shards(): lax.all_gather(aggregate, 'feat', axis=0, tiled=True)  6.47 us
    all_gather x1, blocking collectives, shards(): lax.all_gather(features, 'feat', axis=0, tiled=True)  6.42 us
    ppermute x15, waiting for transfers between devices, shards(): lax.ppermute(sent, 'dom', [(i, i ^ turn) for i in range(devices)])  5.68 us
    dot_general x3, matrix products, tile_terms(): jnp.einsum('fti,tr->fri', partial_value, onehot, precision=lax.Precision....  3.16 us
    gather x3, local copies, waits for them, and re-layouts, tile_terms(): picked = jnp.take(blocks, source, axis=1)  1.94 us
    gather x1, local copies, waits for them, and re-layouts, shards(): hub_blocks = jnp.take(everyone, hub_owner * HOWN + order_rank, axis=1)  1.79 us
  transfers between devices with their start and end apart: 16, of which 3 were waited for; matrix products, arithmetic and copies ran while one was open for 9% of the time, Pallas kernels for 0%

profile of v1, /device:TPU:0, one launch (start us, length us, event | category | flops | bytes accessed | tf_op | source)
XLA Modules:
  0.0 77.4 jit_solution(2698391043795979528)
XLA Ops:
  6.6 0.7 copy-done.14
  7.3 0.2 convert_reduce_fusion
  7.6 0.6 copy-done.7
  8.3 1.0 %copy.61 = bf16[128,512]{0,1:T(8,128)(2,1)S(1)} copy(bf16[128,512]{1,0:T(8,128)(2,1)} %param.22) | data formatting | bytes 262144 | tf_op args[0]
  9.4 0.6 copy-done.13
  10.1 0.9 %gather_fusion.4 = bf16[256,128]{1,0:T(8,128)(2,1)S(1)} fusion(bf16[128,512]{0,1:T(8,128)(2,1)S(1)} %copy.61, s32[1024]{0:T(1024)S(1)} %pad_clamp_fusion.5), kind=kCustom, calls=%fused_computation.1.clone | custom fusion | bytes 132096 | tf_op jit(solution)/shard_map/jit(_take)/gather | solution.py:60
  11.3 0.5 collective-permute-start
  11.8 2.6 %collective-permute-start.1 = (bf16[128,1,16]{0,2,1:T(8,128)(2,1)S(1)}, bf16[128,1,16]{0,2,1:T(8,128)(2,1)S(1)}, u32[]{:S(2)}, u32[]{:S(2)}) collective-permute-start(bf16[128,1,16]{0,2,1:T(8,128)(2,1)S(1)} %get-tuple-element.22), channel_id=1, source_target_pairs={{0,4},{2,6},{4,0},{6,2},{8,12},{10,14},{12,8},{14,10},{16,20},{18,... | collective-permute-start | bytes 12296 | tf_op jit(solution)/shard_map/ppermute | solution.py:70
  14.5 1.8 %collective-permute-start.3 = (bf16[128,1,16]{0,2,1:T(8,128)(2,1)S(1)}, bf16[128,1,16]{0,2,1:T(8,128)(2,1)S(1)}, u32[]{:S(2)}, u32[]{:S(2)}) collective-permute-start(bf16[128,1,16]{0,2,1:T(8,128)(2,1)S(1)} %get-tuple-element.20), channel_id=1, source_target_pairs={{0,8},{2,10},{4,12},{6,14},{8,0},{10,2},{12,4},{14,6},{16,24},{18,... | collective-permute-start | bytes 12296 | tf_op jit(solution)/shard_map/ppermute | solution.py:70
  16.3 0.9 %gather_fusion.5 = bf16[256,128]{1,0:T(8,128)(2,1)S(1)} fusion(bf16[128,512]{0,1:T(8,128)(2,1)S(1)} %copy.61, s32[1024]{0:T(1024)S(1)} %pad_clamp_fusion.2), kind=kCustom, calls=%fused_computation.3.clone | custom fusion | bytes 132096 | tf_op jit(solution)/shard_map/jit(_take)/gather | solution.py:86
  17.3 0.7 copy.68
  18.1 0.6 copy-done.15
  18.7 0.6 copy-done.9
  19.4 0.6 copy-done.16
  20.0 0.1 copy.62
  20.2 0.7 copy-done.8
  20.9 0.6 gather_fusion.3
  21.6 0.5 convolution_bitcast_fusion.2
  22.1 0.1 copy-done.10
  22.2 1.1 %fusion.7 = f32[4,128,128]{2,0,1:T(4,128)S(1)} fusion(f32[128,16,128]{2,0,1:T(8,128)S(1)} %convolution_bitcast_fusion.2, s32[16]{0:T(128)S(1)} %copy-done.10), kind=kOutput, calls=%fused_computation.21 | convolution fusion | flops 12582976 | bytes 1310784 | tf_op jit(solution)/shard_map/fti,tr->fri/dot_general | solution.py:29
  23.3 6.4 %all_gather.9 = bf16[256,512]{1,0:T(8,128)(2,1)S(1)} all-gather(bf16[128,512]{1,0:T(8,128)(2,1)S(1)} %copy-done.3), channel_id=1, replica_groups=mesh['dom'=16,'feat'=2] {'feat'}, dimensions={0}, use_global_device_ids=true | all-gather | bytes 393216 | tf_op jit(solution)/shard_map/all_gather | solution.py:100
  29.7 2.7 %collective-permute-start.5 = (bf16[128,1,16]{0,2,1:T(8,128)(2,1)S(1)}, bf16[128,1,16]{0,2,1:T(8,128)(2,1)S(1)}, u32[]{:S(2)}, u32[]{:S(2)}) collective-permute-start(bf16[128,1,16]{0,2,1:T(8,128)(2,1)S(1)} %get-tuple-element.18), channel_id=1, source_target_pairs={{0,12},{2,14},{4,8},{6,10},{8,4},{10,6},{12,0},{14,2},{16,28},{18,... | collective-permute-start | bytes 12296 | tf_op jit(solution)/shard_map/ppermute | solution.py:70
  32.5 2.7 %collective-permute-start.7 = (bf16[128,1,16]{0,2,1:T(8,128)(2,1)S(1)}, bf16[128,1,16]{0,2,1:T(8,128)(2,1)S(1)}, u32[]{:S(2)}, u32[]{:S(2)}) collective-permute-start(bf16[128,1,16]{0,2,1:T(8,128)(2,1)S(1)} %get-tuple-element.16), channel_id=1, source_target_pairs={{0,16},{2,18},{4,20},{6,22},{8,24},{10,26},{12,28},{14,30},{16,0},... | collective-permute-start | bytes 12296 | tf_op jit(solution)/shard_map/ppermute | solution.py:70
  35.2 0.1 collective-permute-start.8
  35.3 3.5 %collective-permute-start.9 = (bf16[128,1,16]{0,2,1:T(8,128)(2,1)S(1)}, bf16[128,1,16]{0,2,1:T(8,128)(2,1)S(1)}, u32[]{:S(2)}, u32[]{:S(2)}) collective-permute-start(bf16[128,1,16]{0,2,1:T(8,128)(2,1)S(1)} %get-tuple-element.14), channel_id=1, source_target_pairs={{0,20},{2,22},{4,16},{6,18},{8,28},{10,30},{12,24},{14,26},{16,4},... | collective-permute-start | bytes 12296 | tf_op jit(solution)/shard_map/ppermute | solution.py:70
  38.9 2.9 %collective-permute-start.11 = (bf16[128,1,16]{0,2,1:T(8,128)(2,1)S(1)}, bf16[128,1,16]{0,2,1:T(8,128)(2,1)S(1)}, u32[]{:S(2)}, u32[]{:S(2)}) collective-permute-start(bf16[128,1,16]{0,2,1:T(8,128)(2,1)S(1)} %get-tuple-element.12), channel_id=1, source_target_pairs={{0,24},{2,26},{4,28},{6,30},{8,16},{10,18},{12,20},{14,22},{16,8},... | collective-permute-start | bytes 12296 | tf_op jit(solution)/shard_map/ppermute | solution.py:70
  41.8 0.7 collective-permute-start.12
  42.5 4.4 %collective-permute-start.13 = (bf16[128,1,16]{0,2,1:T(8,128)(2,1)S(1)}, bf16[128,1,16]{0,2,1:T(8,128)(2,1)S(1)}, u32[]{:S(2)}, u32[]{:S(2)}) collective-permute-start(bf16[128,1,16]{0,2,1:T(8,128)(2,1)S(1)} %get-tuple-element.10), channel_id=1, source_target_pairs={{0,28},{2,30},{4,24},{6,26},{8,20},{10,22},{12,16},{14,18},{16,12}... | collective-permute-start | bytes 12296 | tf_op jit(solution)/shard_map/ppermute | solution.py:70
  47.1 1.8 %collective-permute-done.13 = bf16[128,1,16]{0,2,1:T(8,128)(2,1)S(1)} collective-permute-done((bf16[128,1,16]{0,2,1:T(8,128)(2,1)S(1)}, bf16[128,1,16]{0,2,1:T(8,128)(2,1)S(1)}, u32[]{:S(2)}, u32[]{:S(2)}) %collective-permute-start.13) | collective-permute-done | bytes 4128 | tf_op jit(solution)/shard_map/ppermute | solution.py:70
  48.9 3.9 %collective-permute-done.14 = bf16[128,1,16]{0,2,1:T(8,128)(2,1)S(1)} collective-permute-done((bf16[128,1,16]{0,2,1:T(8,128)(2,1)S(1)}, bf16[128,1,16]{0,2,1:T(8,128)(2,1)S(1)}, u32[]{:S(2)}, u32[]{:S(2)}) %collective-permute-start.14) | collective-permute-done | bytes 4128 | tf_op jit(solution)/shard_map/ppermute | solution.py:70
  52.8 0.6 gather_fusion
  53.3 0.1 copy.65
  53.5 0.6 gather_fusion.1
  54.1 0.4 copy-done.1
  54.5 0.5 convolution_bitcast_fusion.1
  55.0 0.1 copy-done.11
  55.2 1.1 %convolution_add_fusion.1 = f32[4,128,128]{2,0,1:T(4,128)S(1)} fusion(f32[4,128,128]{2,0,1:T(4,128)S(1)} %fusion.7, f32[128,16,128]{2,0,1:T(8,128)S(1)} %convolution_bitcast_fusion.1, s32[16]{0:T(128)S(1)} %copy-done.11), kind=kOutput, calls=%fused_computation.11 | convolution fusion | flops 12648512 | bytes 1572928 | tf_op jit(solution)/shard_map/fti,tr->fri/dot_general | solution.py:29
  56.2 1.5 %all-gather.2.cloned.1.call-done = bf16[128,32,128]{2,0,1:T(8,128)(2,1)} async-done(((bf16[128,2,128]{2,0,1:T(8,128)(2,1)}), bf16[128,32,128]{2,0,1:T(8,128)(2,1)}) %all-gather.2.cloned.1.call-update) | async-done | bytes 1048592 | tf_op jit(solution)/shard_map/all_gather | solution.py:89
  57.7 1.8 %gather_fusion.2 = bf16[4,128,128]{2,1,0:T(8,128)(2,1)S(1)} fusion(bf16[128,32,128]{2,0,1:T(8,128)(2,1)} %all-gather.2.cloned.1.call-done, s32[1024]{0:T(1024)S(1)} %get-tuple-element.34), kind=kCustom, calls=%fused_computation.6 | custom fusion | bytes 262160 | tf_op jit(solution)/shard_map/jit(_take)/gather | solution.py:90
  59.6 0.6 gather_fusion.6
  60.3 0.4 copy-done.2
  60.6 0.5 convolution_bitcast_fusion
  61.2 0.1 copy-done.17
  61.3 1.1 %fusion.3 = bf16[4,128,128]{2,0,1:T(4,128)(2,1)S(1)} fusion(f32[4,128,128]{2,0,1:T(4,128)S(1)} %convolution_add_fusion.1, f32[128,16,128]{2,0,1:T(8,128)S(1)} %convolution_bitcast_fusion, f32[4,128]{1,0:T(4,128)S(1)} %convert_bitcast_fusion, s32[16]{0:T(128)S(1)} %copy-done.17), kind=kOutput, calls=%fused_computation.17 | convolution fusion | flops 12779584 | bytes 1443904 | tf_op jit(solution)/shard_map/fti,tr->fri/dot_general | solution.py:29
  62.4 6.5 %all_gather.11 = bf16[256,512]{1,0:T(8,128)(2,1)S(1)} all-gather(bf16[128,512]{1,0:T(8,128)(2,1)S(1)} %bitcast.127), channel_id=1, replica_groups=mesh['dom'=16,'feat'=2] {'feat'}, dimensions={0}, use_global_device_ids=true | all-gather | bytes 393216 | tf_op jit(solution)/shard_map/all_gather | solution.py:105
  68.9 0.2 convolution_bitcast_fusion.3
  69.1 0.6 copy-done.5
  69.7 0.8 %fusion.4 = bf16[128,512]{1,0:T(8,128)(2,1)} fusion(f32[128,512]{1,0:T(8,128)S(1)} %convolution_bitcast_fusion.3, bf16[128,256]{1,0:T(8,128)(2,1)S(1)} %copy-done.5, bf16[256,512]{1,0:T(8,128)(2,1)S(1)} %all_gather.9, f32[128]{0:T(128)S(1)} %copy-done.12), kind=kOutput, calls=%fused_computation.18 | convolution fusion | flops 33816576 | bytes 721408 | tf_op jit(solution)/shard_map/dot_general | solution.py:98
  (84 shorter events, 1.1 us)
Async XLA Ops:
  6.5 15.0 %copy-start = (bf16[16,128,128]{2,1,0:T(8,128)(2,1)S(1)}, bf16[16,128,128]{2,1,0:T(8,128)(2,1)}, u32[]{:S(2)}) copy-start(bf16[16,128,128]{2,1,0:T(8,128)(2,1)} %param.30) | copy-start | bytes 1572868
  6.5 0.7 copy-start.14
  6.5 0.9 %copy-start.6 = (s32[1,16,16]{2,1,0:T(8,128)S(1)}, s32[1,16,16]{2,1,0:T(8,128)}, u32[]{:S(2)}) copy-start(s32[1,16,16]{2,1,0:T(8,128)} %param.24) | copy-start | bytes 3076
  6.5 51.2 %all-gather.2.cloned.1.call-start = ((), (), s32[]{:S(2)}) async-start(), calls=%async_computation | async-start | bytes 1114112 | tf_op jit(solution)/shard_map/all_gather | solution.py:89
  7.5 0.7 copy-start.7
  9.4 0.7 copy-start.13
  11.3 18.4 %collective-permute-start = (bf16[128,1,16]{0,2,1:T(8,128)(2,1)S(1)}, bf16[128,1,16]{0,2,1:T(8,128)(2,1)S(1)}, u32[]{:S(2)}, u32[]{:S(2)}) collective-permute-start(bf16[128,1,16]{0,2,1:T(8,128)(2,1)S(1)} %get-tuple-element.23), channel_id=1, source_target_pairs={{0,2},{2,0},{4,6},{6,4},{8,10},{10,8},{12,14},{14,12},{16,18},{18,... | collective-permute-start | bytes 12296 | tf_op jit(solution)/shard_map/ppermute | solution.py:70
  11.8 20.6 %collective-permute-start.1 = (bf16[128,1,16]{0,2,1:T(8,128)(2,1)S(1)}, bf16[128,1,16]{0,2,1:T(8,128)(2,1)S(1)}, u32[]{:S(2)}, u32[]{:S(2)}) collective-permute-start(bf16[128,1,16]{0,2,1:T(8,128)(2,1)S(1)} %get-tuple-element.22), channel_id=1, source_target_pairs={{0,4},{2,6},{4,0},{6,2},{8,12},{10,14},{12,8},{14,10},{16,20},{18,... | collective-permute-start | bytes 12296 | tf_op jit(solution)/shard_map/ppermute | solution.py:70
  14.4 18.1 %collective-permute-start.2 = (bf16[128,1,16]{0,2,1:T(8,128)(2,1)S(1)}, bf16[128,1,16]{0,2,1:T(8,128)(2,1)S(1)}, u32[]{:S(2)}, u32[]{:S(2)}) collective-permute-start(bf16[128,1,16]{0,2,1:T(8,128)(2,1)S(1)} %get-tuple-element.21), channel_id=1, source_target_pairs={{0,6},{2,4},{4,2},{6,0},{8,14},{10,12},{12,10},{14,8},{16,22},{18,... | collective-permute-start | bytes 12296 | tf_op jit(solution)/shard_map/ppermute | solution.py:70
  14.5 20.7 %collective-permute-start.3 = (bf16[128,1,16]{0,2,1:T(8,128)(2,1)S(1)}, bf16[128,1,16]{0,2,1:T(8,128)(2,1)S(1)}, u32[]{:S(2)}, u32[]{:S(2)}) collective-permute-start(bf16[128,1,16]{0,2,1:T(8,128)(2,1)S(1)} %get-tuple-element.20), channel_id=1, source_target_pairs={{0,8},{2,10},{4,12},{6,14},{8,0},{10,2},{12,4},{14,6},{16,24},{18,... | collective-permute-start | bytes 12296 | tf_op jit(solution)/shard_map/ppermute | solution.py:70
  16.3 19.0 %collective-permute-start.4 = (bf16[128,1,16]{0,2,1:T(8,128)(2,1)S(1)}, bf16[128,1,16]{0,2,1:T(8,128)(2,1)S(1)}, u32[]{:S(2)}, u32[]{:S(2)}) collective-permute-start(bf16[128,1,16]{0,2,1:T(8,128)(2,1)S(1)} %get-tuple-element.19), channel_id=1, source_target_pairs={{0,10},{2,8},{4,14},{6,12},{8,2},{10,0},{12,6},{14,4},{16,26},{18,... | collective-permute-start | bytes 12296 | tf_op jit(solution)/shard_map/ppermute | solution.py:70
  18.0 0.7 copy-start.15
  18.7 0.7 copy-start.9
  19.4 0.7 copy-start.16
  20.2 0.7 copy-start.8
  21.6 0.7 copy-start.10
  22.2 1.1 %copy-start.3 = (bf16[128,512]{1,0:T(8,128)(2,1)S(1)}, bf16[128,512]{1,0:T(8,128)(2,1)}, u32[]{:S(2)}) copy-start(bf16[128,512]{1,0:T(8,128)(2,1)} %param.22) | copy-start | bytes 393220
  29.7 9.1 %collective-permute-start.5 = (bf16[128,1,16]{0,2,1:T(8,128)(2,1)S(1)}, bf16[128,1,16]{0,2,1:T(8,128)(2,1)S(1)}, u32[]{:S(2)}, u32[]{:S(2)}) collective-permute-start(bf16[128,1,16]{0,2,1:T(8,128)(2,1)S(1)} %get-tuple-element.18), channel_id=1, source_target_pairs={{0,12},{2,14},{4,8},{6,10},{8,4},{10,6},{12,0},{14,2},{16,28},{18,... | collective-permute-start | bytes 12296 | tf_op jit(solution)/shard_map/ppermute | solution.py:70
  32.5 6.4 %collective-permute-start.6 = (bf16[128,1,16]{0,2,1:T(8,128)(2,1)S(1)}, bf16[128,1,16]{0,2,1:T(8,128)(2,1)S(1)}, u32[]{:S(2)}, u32[]{:S(2)}) collective-permute-start(bf16[128,1,16]{0,2,1:T(8,128)(2,1)S(1)} %get-tuple-element.17), channel_id=1, source_target_pairs={{0,14},{2,12},{4,10},{6,8},{8,6},{10,4},{12,2},{14,0},{16,30},{18,... | collective-permute-start | bytes 12296 | tf_op jit(solution)/shard_map/ppermute | solution.py:70
  32.5 9.3 %collective-permute-start.7 = (bf16[128,1,16]{0,2,1:T(8,128)(2,1)S(1)}, bf16[128,1,16]{0,2,1:T(8,128)(2,1)S(1)}, u32[]{:S(2)}, u32[]{:S(2)}) collective-permute-start(bf16[128,1,16]{0,2,1:T(8,128)(2,1)S(1)} %get-tuple-element.16), channel_id=1, source_target_pairs={{0,16},{2,18},{4,20},{6,22},{8,24},{10,26},{12,28},{14,30},{16,0},... | collective-permute-start | bytes 12296 | tf_op jit(solution)/shard_map/ppermute | solution.py:70
  35.2 7.4 %collective-permute-start.8 = (bf16[128,1,16]{0,2,1:T(8,128)(2,1)S(1)}, bf16[128,1,16]{0,2,1:T(8,128)(2,1)S(1)}, u32[]{:S(2)}, u32[]{:S(2)}) collective-permute-start(bf16[128,1,16]{0,2,1:T(8,128)(2,1)S(1)} %get-tuple-element.15), channel_id=1, source_target_pairs={{0,18},{2,16},{4,22},{6,20},{8,26},{10,24},{12,30},{14,28},{16,2},... | collective-permute-start | bytes 12296 | tf_op jit(solution)/shard_map/ppermute | solution.py:70
  35.3 11.7 %collective-permute-start.9 = (bf16[128,1,16]{0,2,1:T(8,128)(2,1)S(1)}, bf16[128,1,16]{0,2,1:T(8,128)(2,1)S(1)}, u32[]{:S(2)}, u32[]{:S(2)}) collective-permute-start(bf16[128,1,16]{0,2,1:T(8,128)(2,1)S(1)} %get-tuple-element.14), channel_id=1, source_target_pairs={{0,20},{2,22},{4,16},{6,18},{8,28},{10,30},{12,24},{14,26},{16,4},... | collective-permute-start | bytes 12296 | tf_op jit(solution)/shard_map/ppermute | solution.py:70
  38.8 8.2 %collective-permute-start.10 = (bf16[128,1,16]{0,2,1:T(8,128)(2,1)S(1)}, bf16[128,1,16]{0,2,1:T(8,128)(2,1)S(1)}, u32[]{:S(2)}, u32[]{:S(2)}) collective-permute-start(bf16[128,1,16]{0,2,1:T(8,128)(2,1)S(1)} %get-tuple-element.13), channel_id=1, source_target_pairs={{0,22},{2,20},{4,18},{6,16},{8,30},{10,28},{12,26},{14,24},{16,6},... | collective-permute-start | bytes 12296 | tf_op jit(solution)/shard_map/ppermute | solution.py:70
  38.9 8.2 %collective-permute-start.11 = (bf16[128,1,16]{0,2,1:T(8,128)(2,1)S(1)}, bf16[128,1,16]{0,2,1:T(8,128)(2,1)S(1)}, u32[]{:S(2)}, u32[]{:S(2)}) collective-permute-start(bf16[128,1,16]{0,2,1:T(8,128)(2,1)S(1)} %get-tuple-element.12), channel_id=1, source_target_pairs={{0,24},{2,26},{4,28},{6,30},{8,16},{10,18},{12,20},{14,22},{16,8},... | collective-permute-start | bytes 12296 | tf_op jit(solution)/shard_map/ppermute | solution.py:70
  41.8 5.2 %collective-permute-start.12 = (bf16[128,1,16]{0,2,1:T(8,128)(2,1)S(1)}, bf16[128,1,16]{0,2,1:T(8,128)(2,1)S(1)}, u32[]{:S(2)}, u32[]{:S(2)}) collective-permute-start(bf16[128,1,16]{0,2,1:T(8,128)(2,1)S(1)} %get-tuple-element.11), channel_id=1, source_target_pairs={{0,26},{2,24},{4,30},{6,28},{8,18},{10,16},{12,22},{14,20},{16,10}... | collective-permute-start | bytes 12296 | tf_op jit(solution)/shard_map/ppermute | solution.py:70
  42.5 6.3 %collective-permute-start.13 = (bf16[128,1,16]{0,2,1:T(8,128)(2,1)S(1)}, bf16[128,1,16]{0,2,1:T(8,128)(2,1)S(1)}, u32[]{:S(2)}, u32[]{:S(2)}) collective-permute-start(bf16[128,1,16]{0,2,1:T(8,128)(2,1)S(1)} %get-tuple-element.10), channel_id=1, source_target_pairs={{0,28},{2,30},{4,24},{6,26},{8,20},{10,22},{12,16},{14,18},{16,12}... | collective-permute-start | bytes 12296 | tf_op jit(solution)/shard_map/ppermute | solution.py:70
  47.0 5.7 %collective-permute-start.14 = (bf16[128,1,16]{0,2,1:T(8,128)(2,1)S(1)}, bf16[128,1,16]{0,2,1:T(8,128)(2,1)S(1)}, u32[]{:S(2)}, u32[]{:S(2)}) collective-permute-start(bf16[128,1,16]{0,2,1:T(8,128)(2,1)S(1)} %get-tuple-element.9), channel_id=1, source_target_pairs={{0,30},{2,28},{4,26},{6,24},{8,22},{10,20},{12,18},{14,16},{16,14}... | collective-permute-start | bytes 12296 | tf_op jit(solution)/shard_map/ppermute | solution.py:70
  53.4 1.1 %copy-start.1 = (bf16[16,128,128]{2,1,0:T(8,128)(2,1)S(1)}, bf16[16,128,128]{2,1,0:T(8,128)(2,1)}, u32[]{:S(2)}) copy-start(bf16[16,128,128]{2,1,0:T(8,128)(2,1)} %param.33) | copy-start | bytes 1572868
  54.5 0.7 copy-start.11
  59.6 1.0 %copy-start.2 = (bf16[16,128,128]{2,1,0:T(8,128)(2,1)S(1)}, bf16[16,128,128]{2,1,0:T(8,128)(2,1)}, u32[]{:S(2)}) copy-start(bf16[16,128,128]{2,1,0:T(8,128)(2,1)} %param.36) | copy-start | bytes 1572868
  60.6 0.7 copy-start.17
  62.4 6.5 %copy-start.4 = (bf16[128,256]{1,0:T(8,128)(2,1)S(1)}, bf16[128,256]{1,0:T(8,128)(2,1)}, u32[]{:S(2)}) copy-start(bf16[128,256]{1,0:T(8,128)(2,1)} %param.38) | copy-start | bytes 196612
  68.9 0.8 %copy-start.5 = (bf16[128,256]{1,0:T(8,128)(2,1)S(1)}, bf16[128,256]{1,0:T(8,128)(2,1)}, u32[]{:S(2)}) copy-start(bf16[128,256]{1,0:T(8,128)(2,1)} %param.37) | copy-start | bytes 196612
  68.9 0.8 %copy-start.12 = (f32[128]{0:T(128)S(1)}, f32[128]{0:T(128)}, u32[]{:S(2)}) copy-start(f32[128]{0:T(128)} %param.39) | copy-start | bytes 1540
Sparse Core Ops, SparseCore 0:
  18.2 39.4 all-gather.1
